TPU v7x, 32 devices: a whole 2x2x4 slice. The times are simulated.
32 devices in a mesh: slab: 8 (over z, y), rays: 4 (over x, core).
Axes of the slice: x: 2, y: 2, z: 4, core: 2. Of those that a mesh axis runs over, the one named last changes fastest.
Arguments:
- geometry: float32 [6, 4, 128], P(None, 'rays'), may hold values from -1 to 1
- entry: int32 [8, 4, 128], P('slab', 'rays'), may hold values from 0 to 63
- counts: int32 [8, 4, 128], P('slab', 'rays'), may hold values from 0 to 8
- targets: float32 [3, 4, 128], P(None, 'rays', 'slab'), may hold values from 0 to 1
- w_in: float32 [8, 256, 256], P('slab'), may hold values from -0.375 to 0.375
- w_mid: float32 [8, 2, 256, 256], P('slab'), may hold values from -0.375 to 0.375
- w_out: float32 [8, 4, 256], P('slab'), may hold values from -0.375 to 0.375
- b_hid: float32 [8, 3, 256], P('slab'), may hold values from -3 to 3
- b_out: float32 [8, 4], P('slab'), may hold values from -3 to 3
- freqs: float32 [8, 3, 128], P('slab'), may hold values from -3 to 3
Outputs:
- pixels: float32 [3, 4, 128], P(None, 'rays', 'slab')
- grad_in: float32 [8, 256, 256], P('slab')
- grad_mid: float32 [8, 2, 256, 256], P('slab')
- grad_out: float32 [8, 4, 256], P('slab')
- grad_hid: float32 [8, 3, 256], P('slab')
- grad_bout: float32 [8, 4], P('slab')
Inputs may be any that keep to these rules, and one draw needn't show every extreme that they name: `entry`: the index of a ray's first sample in a slab. `counts`: how many of the 8 slots of a ray lie inside a slab; 0 where the ray misses it.
All inputs are finite; a program needn't handle non-finite values.
Results may differ from a plain program's by a relative error of at most 0.0003.
Values sent between devices are 32-bit elements; how exact they have to be, the bound alone decides.
A program may use at most 128 MiB of HBM per device.

v0:
```python
import math
import jax
import jax.numpy as jnp
from jax import lax
from jax.sharding import PartitionSpec as P

MID = 2
SAMP = 8
RAY_DEV = 16
HIGH = lax.Precision.HIGHEST


def features(freqs, geometry, entry):
    width = geometry.shape[1]
    slots = jnp.arange(SAMP, dtype=jnp.int32)[:, None]
    times = 0.25 * (entry.astype(jnp.float32)[None, :] + slots.astype(jnp.float32) + 0.5)
    places = geometry[0:3, None, :] + times[None] * geometry[3:6, None, :]
    places = places.reshape(3, SAMP * width)
    phase = jnp.einsum("dk,dn->nk", freqs, places, precision=HIGH)
    return jnp.concatenate([jnp.sin(phase), jnp.cos(phase)], axis=1)


def hidden_layer(hidden, weight, bias):
    return jax.nn.softplus(jnp.dot(hidden, weight, precision=HIGH) + bias)


def head(hidden, w_out, b_out, counts, delta):
    width = counts.shape[0]
    slots = jnp.arange(SAMP, dtype=jnp.int32)[:, None]
    result = jnp.einsum("ch,nh->cn", w_out, hidden, precision=HIGH) + b_out[:, None]
    sigma = jax.nn.softplus(result[0]).reshape(SAMP, width)
    colors = jax.nn.sigmoid(result[1:]).reshape(3, SAMP, width)
    alive = slots < counts[None, :]
    depth = jnp.where(alive, sigma * delta, jnp.float32(0.0))
    before = jnp.cumsum(depth, axis=0) - depth
    weights = jnp.exp(-before) * (1.0 - jnp.exp(-depth))
    color = jnp.sum(weights[None] * colors, axis=1)
    logtrans = -jnp.sum(depth, axis=0)
    return jnp.concatenate([color, logtrans[None]], axis=0)


def segment(params, encoded, counts, delta):
    hidden = hidden_layer(encoded, params[0], params[3][0])
    for layer in range(MID):
        hidden = hidden_layer(hidden, params[1][layer], params[3][layer + 1])
    return head(hidden, params[2], params[4], counts, delta)


def composite(segments, targets, factor):
    logtrans = segments[3]
    before = jnp.cumsum(logtrans, axis=0) - logtrans
    shade = jnp.exp(before)
    pixels = jnp.sum(shade[None] * segments[:3], axis=1) + jnp.exp(jnp.sum(logtrans, axis=0))[None]
    loss = factor * jnp.sum((pixels - targets) ** 2)
    return (loss, pixels)


def shards(geometry, entry, counts, targets, w_in, w_mid, w_out, b_hid, b_out, freqs):
    slabs = lax.axis_size("slab")
    delta = 3.0 / (SAMP * slabs)
    factor = 1.0 / math.sqrt(3.0 * lax.axis_size("rays") * slabs * RAY_DEV)
    local_geometry = geometry[:, 0, :]
    local_entry = entry[0, 0]
    local_counts = counts[0, 0]
    local_targets = targets[:, 0, :]
    params = (w_in[0], w_mid[0], w_out[0], b_hid[0], b_out[0])
    encoded = features(freqs[0], local_geometry, local_entry)
    seg, pull_all = jax.vjp(lambda p: segment(p, encoded, local_counts, delta), params)
    owned = lax.all_to_all(seg[:, None, :], "slab", split_axis=2, concat_axis=1, tiled=True)
    loss, pullback, pixels = jax.vjp(
        lambda s: composite(s, local_targets, factor), owned, has_aux=True
    )
    owned_adjoint = pullback(jnp.ones((), jnp.float32))[0]
    adjoint = lax.all_to_all(owned_adjoint, "slab", split_axis=1, concat_axis=2, tiled=True)[
        :, 0, :
    ]
    grads = pull_all(adjoint)[0]
    grad_in, grad_mid, grad_out, grad_hid, grad_bout = lax.psum(
        (grads[0], grads[1], grads[2], grads[3], grads[4]), "rays"
    )
    return (
        pixels[:, None, :],
        grad_in[None],
        grad_mid[None],
        grad_out[None],
        grad_hid[None],
        grad_bout[None],
    )


def solution(mesh):
    in_specs = (
        P(None, "rays", None),
        P("slab", "rays", None),
        P("slab", "rays", None),
        P(None, "rays", "slab"),
        P("slab", None, None),
        P("slab", None, None, None),
        P("slab", None, None),
        P("slab", None, None),
        P("slab", None),
        P("slab", None, None),
    )
    out_specs = (
        P(None, "rays", "slab"),
        P("slab", None, None),
        P("slab", None, None, None),
        P("slab", None, None),
        P("slab", None, None),
        P("slab", None),
    )
    return jax.shard_map(shards, mesh=mesh, in_specs=in_specs, out_specs=out_specs, check_vma=False)
```

profile of v0, /device:TPU:0, one launch (start us, length us, event | category | flops | bytes accessed | tf_op | source)
XLA Modules:
  0.0 106.8 jit_solution(6340818017745772977)
XLA Ops:
  7.2 0.7 copy-done.9
  7.9 0.7 copy-done.3
  8.7 0.7 copy-done.4
  9.4 5.2 %fusion.69 = (f32[1024,128]{0,1:T(8,128)S(1)}, f32[1024,128]{0,1:T(8,128)S(1)}) fusion(f32[1,3,128]{2,0,1:T(1,128)S(1)} %copy-done.4, f32[1,3,8,128]{3,2,1,0:T(8,128)S(1)} %add_bitcast_fusion.1), kind=kOutput, calls=%fused_computation.129 | convolution fusion | flops 4718592 | bytes 1062400 | tf_op jit(solution)/shard_map/dk,dn->nk/dot_general | solution.py:19
  14.6 1.8 %convolution_add_fusion.2 = f32[1024,256]{1,0:T(8,128)S(1)} fusion(f32[1024,128]{0,1:T(8,128)S(1)} %get-tuple-element.64, f32[1024,128]{0,1:T(8,128)S(1)} %get-tuple-element.63, f32[256]{0:T(256)S(1)} %bitcast.147, f32[1,256,256]{2,1,0:T(8,128)S(1)} %copy-done), kind=kOutput, calls=%fused_computation.14 | convolution fusion | flops 805830656 | bytes 2360320 | tf_op jit(solution)/shard_map/jvp()/dot_general | solution.py:24
  16.4 1.4 %convolution_add_fusion.1 = f32[1024,256]{1,0:T(8,128)S(1)} fusion(f32[1024,256]{1,0:T(8,128)S(1)} %convolution_add_fusion.2, f32[256]{0:T(256)S(1)} %bitcast.156, f32[1,2,256,256]{3,2,1,0:T(8,128)S(1)} %copy-done.7), kind=kOutput, calls=%fused_computation.13 | convolution fusion | flops 807141376 | bytes 2360320 | tf_op jit(solution)/shard_map/jvp()/dot_general | solution.py:24
  17.9 1.5 %convolution_add_fusion = f32[1024,256]{1,0:T(8,128)S(1)} fusion(f32[1024,256]{1,0:T(8,128)S(1)} %convolution_add_fusion.1, f32[256]{0:T(256)S(1)} %bitcast.155, f32[1,2,256,256]{3,2,1,0:T(8,128)S(1)} %copy-done.7), kind=kOutput, calls=%fused_computation.12 | convolution fusion | flops 807141376 | bytes 2360320 | tf_op jit(solution)/shard_map/jvp()/dot_general | solution.py:24
  19.4 0.7 copy-done.10
  20.0 1.5 %fusion = f32[4,1024]{1,0:T(4,128)S(1)} fusion(f32[1024,256]{1,0:T(8,128)S(1)} %convolution_add_fusion, f32[4]{0:T(128)S(1)} %bitcast.157, f32[1,4,256]{2,1,0:T(4,128)S(1)} %copy-done.8), kind=kOutput, calls=%fused_computation.19 | convolution fusion | flops 14159872 | bytes 1069072 | tf_op jit(solution)/shard_map/jvp(ch,nh->cn)/dot_general | solution.py:30
  21.6 0.6 copy-done.5
  22.4 0.8 copy.29
  23.1 7.3 %all-to-all-start = ((f32[4,1,128]{0,1,2:T(1,128)}), f32[4,1,128]{0,1,2:T(1,128)S(1)}, u32[]{:S(2)}, u32[]{:S(2)}) async-start(f32[4,1,128]{0,1,2:T(1,128)} %bitcast.13), calls=%async_computation | async-start | bytes 131072 | tf_op jit(solution)/shard_map/all_to_all | solution.py:69
  30.5 6.9 %all-to-all-done = f32[4,1,128]{0,1,2:T(1,128)S(1)} async-done(((f32[4,1,128]{0,1,2:T(1,128)}), f32[4,1,128]{0,1,2:T(1,128)S(1)}, u32[]{:S(2)}, u32[]{:S(2)}) %all-to-all-start) | async-done | bytes 2080 | tf_op jit(solution)/shard_map/all_to_all | solution.py:69
  37.3 1.8 %slice_reduce_fusion = f32[128]{0:T(128)S(1)} fusion(f32[4,1,128]{0,1,2:T(1,128)S(1)} %all-to-all-done), kind=kLoop, calls=%fused_computation.44 | loop fusion | bytes 1024 | tf_op jit(solution)/shard_map/jvp()/slice | solution.py:50
  39.6 0.7 copy-done.6
  40.6 0.6 copy.31
  41.2 3.3 %all-to-all-start.1 = ((f32[4,8,16]{2,0,1:T(4,128)}), f32[4,8,16]{2,0,1:T(4,128)S(1)}, u32[]{:S(2)}, u32[]{:S(2)}) async-start(f32[4,8,16]{2,0,1:T(4,128)} %copy.31), calls=%async_computation.1 | async-start | bytes 32768 | tf_op jit(solution)/shard_map/all_to_all | solution.py:74
  44.5 0.2 all-reduce.13.cloned.1.call-start
  44.8 6.3 %all-to-all-done.1 = f32[4,8,16]{2,0,1:T(4,128)S(1)} async-done(((f32[4,8,16]{2,0,1:T(4,128)}), f32[4,8,16]{2,0,1:T(4,128)S(1)}, u32[]{:S(2)}, u32[]{:S(2)}) %all-to-all-start.1) | async-done | bytes 2080 | tf_op jit(solution)/shard_map/all_to_all | solution.py:74
  51.4 3.0 %fusion.75 = (f32[256]{0:T(256)S(1)}, f32[1024,256]{1,0:T(8,128)S(1)}) fusion(f32[1024,256]{1,0:T(8,128)} %copy-done.13, f32[1,4,256]{2,1,0:T(4,128)S(1)} %copy-done.8, f32[1,1024]{1,0:T(1,128)S(1)} %fusion.36, f32[3,1024]{1,0:T(4,128)S(1)} %get-tuple-element.65), kind=kOutput, calls=%fused_computation.135 | convolution fusion | flops 15994624 | bytes 2118656 | tf_op jit(solution)/shard_map/transpose(jvp(ch,nh->cn))/dot_general | solution.py:30
  54.5 2.3 %convolution_bitcast_fusion.1 = f32[1,256,256]{2,1,0:T(8,128)S(1)} fusion(f32[1024,256]{1,0:T(8,128)S(1)} %get-tuple-element.80, f32[1024,256]{1,0:T(8,128)S(1)} %copy-done.12), kind=kOutput, calls=%fused_computation.16 | convolution fusion | flops 806879232 | bytes 2359296 | tf_op jit(solution)/shard_map/transpose(jvp())/dot_general | solution.py:24
  56.7 1.7 %fusion.74 = (f32[256]{0:T(256)S(1)}, f32[1024,256]{1,0:T(8,128)S(1)}) fusion(f32[1024,256]{1,0:T(8,128)S(1)} %copy-done.12, f32[1024,256]{1,0:T(8,128)S(1)} %get-tuple-element.80, f32[1,2,256,256]{3,2,1,0:T(8,128)S(1)} %copy-done.7), kind=kOutput, calls=%fused_computation.134 | convolution fusion | flops 808713984 | bytes 3408896 | tf_op jit(solution)/shard_map/transpose(jvp())/dot_general | solution.py:24
  58.4 2.3 %convolution_bitcast_fusion = f32[1,256,256]{2,1,0:T(8,128)S(1)} fusion(f32[1024,256]{1,0:T(8,128)S(1)} %get-tuple-element.78, f32[1024,256]{1,0:T(8,128)S(1)} %convolution_add_fusion.2), kind=kOutput, calls=%fused_computation.15 | convolution fusion | flops 806879232 | bytes 2359296 | tf_op jit(solution)/shard_map/transpose(jvp())/dot_general | solution.py:24
  60.7 1.7 %fusion.73 = (f32[256]{0:T(256)S(1)}, f32[1024,256]{1,0:T(8,128)S(1)}) fusion(f32[1024,256]{1,0:T(8,128)S(1)} %convolution_add_fusion.2, f32[1024,256]{1,0:T(8,128)S(1)} %get-tuple-element.78, f32[1,2,256,256]{3,2,1,0:T(8,128)S(1)} %copy-done.7), kind=kOutput, calls=%fused_computation.133 | convolution fusion | flops 808713984 | bytes 3408896 | tf_op jit(solution)/shard_map/transpose(jvp())/dot_general | solution.py:24
  62.4 1.7 %convolution_bitcast_fusion.2 = f32[1,256,256]{2,1,0:T(8,128)} fusion(f32[1024,256]{1,0:T(8,128)S(1)} %get-tuple-element.76, f32[1024,128]{0,1:T(8,128)S(1)} %get-tuple-element.64, f32[1024,128]{0,1:T(8,128)S(1)} %get-tuple-element.63), kind=kOutput, calls=%fused_computation.17 | convolution fusion | flops 805568512 | bytes 2359296 | tf_op jit(solution)/shard_map/transpose(jvp())/dot_general | solution.py:24
  64.1 0.8 add_bitcast_fusion
  65.0 0.6 copy.33
  65.7 1.1 convolution_bitcast_fusion.3
  66.7 6.9 %all-reduce.9 = (f32[1,4,256]{2,1,0:T(4,128)}, f32[1,3,256]{2,0,1:T(1,128)}, f32[1,4]{1,0:T(1,128)}) all-reduce(f32[1,4,256]{2,1,0:T(4,128)S(1)} %convolution_bitcast_fusion.3, f32[1,3,256]{2,0,1:T(1,128)S(1)} %broadcast_in_dim.83, f32[1,4]{1,0:T(1,128)S(1)} %bitcast.151), channel_id=1, replica_groups=mesh['slab'=8,'rays'=4] {'rays'}, use_global_device_ids=true, to_apply=%region_13.15 | all-reduce | flops 1796 | bytes 14368 | tf_op jit(solution)/shard_map/psum | solution.py:78
  73.7 23.7 %all-reduce.13.cloned.1.call-done = (f32[1,256,256]{2,1,0:T(8,128)}, f32[1,2,256,256]{3,2,1,0:T(8,128)}) async-done(((f32[1,256,256]{2,1,0:T(8,128)}, f32[1,2,256,256]{3,2,1,0:T(8,128)}), (f32[1,256,256]{2,1,0:T(8,128)}, f32[1,2,256,256]{3,2,1,0:T(8,128)})) %all-reduce.13.cloned.1.call-update) | async-done | bytes 786448 | tf_op jit(solution)/shard_map/psum | solution.py:78
  97.4 1.7 %copy.76 = f32[1,256,256]{2,1,0:T(8,128)} copy(f32[1,256,256]{2,1,0:T(8,128)} %get-tuple-element.84) | data formatting | bytes 524288
  99.1 0.8 copy.77
  (75 shorter events, 1.5 us)
Async XLA Ops:
  7.2 7.4 %copy-start = (f32[1,256,256]{2,1,0:T(8,128)S(1)}, f32[1,256,256]{2,1,0:T(8,128)}, u32[]{:S(2)}) copy-start(f32[1,256,256]{2,1,0:T(8,128)} %param.15) | copy-start | bytes 786436
  7.2 0.7 copy-start.9
  7.2 0.7 copy-start.2
  7.9 0.7 copy-start.3
  8.7 0.7 copy-start.4
  14.5 1.8 %copy-start.7 = (f32[1,2,256,256]{3,2,1,0:T(8,128)S(1)}, f32[1,2,256,256]{3,2,1,0:T(8,128)}, u32[]{:S(2)}) copy-start(f32[1,2,256,256]{3,2,1,0:T(8,128)} %param.16) | copy-start | bytes 1572868
  17.8 1.5 %copy-start.11 = (f32[1024,256]{1,0:T(8,128)}, f32[1024,256]{1,0:T(8,128)S(1)}, u32[]{:S(2)}) copy-start(f32[1024,256]{1,0:T(8,128)S(1)} %convolution_add_fusion.1) | copy-start | bytes 3145732
  17.9 1.5 %copy-start.8 = (f32[1,4,256]{2,1,0:T(4,128)S(1)}, f32[1,4,256]{2,1,0:T(4,128)}, u32[]{:S(2)}) copy-start(f32[1,4,256]{2,1,0:T(4,128)} %param.17) | copy-start | bytes 12292
  19.3 2.2 %copy-start.13 = (f32[1024,256]{1,0:T(8,128)}, f32[1024,256]{1,0:T(8,128)S(1)}, u32[]{:S(2)}) copy-start(f32[1024,256]{1,0:T(8,128)S(1)} %convolution_add_fusion) | copy-start | bytes 3145732
  19.3 0.7 copy-start.10
  21.6 0.7 copy-start.5
  23.1 14.2 %all-to-all-start = ((f32[4,1,128]{0,1,2:T(1,128)}), f32[4,1,128]{0,1,2:T(1,128)S(1)}, u32[]{:S(2)}, u32[]{:S(2)}) async-start(f32[4,1,128]{0,1,2:T(1,128)} %bitcast.13), calls=%async_computation | async-start | bytes 131072 | tf_op jit(solution)/shard_map/all_to_all | solution.py:69
  39.6 0.7 copy-start.6
  41.2 9.9 %all-to-all-start.1 = ((f32[4,8,16]{2,0,1:T(4,128)}), f32[4,8,16]{2,0,1:T(4,128)S(1)}, u32[]{:S(2)}, u32[]{:S(2)}) async-start(f32[4,8,16]{2,0,1:T(4,128)} %copy.31), calls=%async_computation.1 | async-start | bytes 32768 | tf_op jit(solution)/shard_map/all_to_all | solution.py:74
  44.5 52.9 %all-reduce.13.cloned.1.call-start = ((), (), s32[]{:S(2)}) async-start(), calls=%async_computation.2 | async-start | bytes 1572864 | tf_op jit(solution)/shard_map/psum | solution.py:78
  51.4 3.0 %copy-start.12 = (f32[1024,256]{1,0:T(8,128)S(1)}, f32[1024,256]{1,0:T(8,128)}, u32[]{:S(2)}) copy-start(f32[1024,256]{1,0:T(8,128)} %copy-done.11) | copy-start | bytes 3145732
  64.1 1.6 %copy-start.14 = (f32[1024,256]{1,0:T(8,128)S(1)}, f32[1024,256]{1,0:T(8,128)}, u32[]{:S(2)}) copy-start(f32[1024,256]{1,0:T(8,128)} %copy-done.13) | copy-start | bytes 3145732
  97.4 1.7 %copy-start.1 = (f32[1,2,256,256]{3,2,1,0:T(8,128)S(1)}, f32[1,2,256,256]{3,2,1,0:T(8,128)}, u32[]{:S(2)}) copy-start(f32[1,2,256,256]{3,2,1,0:T(8,128)} %get-tuple-element.85) | copy-start | bytes 1572868
Sparse Core Ops, SparseCore 0:
  65.1 32.2 all-reduce.12
where the time goes:
time: 107 us
  waiting for transfers between devices  36.9 us (34%)
  matrix products  25.1 us (23%)
  between operations  14.4 us (13%)
  local copies, waits for them, and re-layouts  11.1 us (10%)
  starting transfers between devices  10.9 us (10%)
  blocking collectives  6.95 us (6%)
  other arithmetic  1.54 us (1%)
    psum x1, waiting for transfers between devices, shards(): lax.psum((grads[0], grads[1], grads[2], grads[3], grads[4]), 'rays')  23.7 us
    dot_general x8, matrix products, hidden_layer(): return jax.nn.softplus(jnp.dot(hidden, weight, precision=HIGH) + bias)  14.3 us
    all_to_all x1, starting transfers between devices, shards(): lax.all_to_all(seg[:, None, :], 'slab', split_axis=2, concat_axis=1, tile...  7.31 us
    unnamed x36, local copies, waits for them, and re-layouts  7.28 us
    psum x1, blocking collectives, shards(): lax.psum((grads[0], grads[1], grads[2], grads[3], grads[4]), 'rays')  6.95 us
    all_to_all x1, waiting for transfers between devices, shards(): lax.all_to_all(seg[:, None, :], 'slab', split_axis=2, concat_axis=1, tile...  6.88 us
    all_to_all x1, waiting for transfers between devices, shards(): lax.all_to_all(owned_adjoint, 'slab', split_axis=1, concat_axis=2, tiled=...  6.27 us
    dot_general x3, matrix products, head(): jnp.einsum('ch,nh->cn', w_out, hidden, precision=HIGH) + b_out[:, None]  5.6 us
  transfers between devices with their start and end apart: 3, of which 3 were waited for; matrix products, arithmetic and copies ran while one was open for 2% of the time, Pallas kernels for 0%

commit v1 on v0

--- a/solution.py
+++ b/solution.py
@@ -8,6 +8,13 @@
 SAMP = 8
 RAY_DEV = 16
 HIGH = lax.Precision.HIGHEST
+
+
+def stacked_exchange(x, axis, split, join):
+    size = lax.axis_size(axis)
+    pieces = jnp.stack(jnp.split(x, size, axis=split), axis=0)
+    pieces = lax.all_to_all(pieces, axis, split_axis=0, concat_axis=0)
+    return jnp.concatenate(pieces, axis=join)
 
 
 def features(freqs, geometry, entry):
@@ -71,9 +78,7 @@
         lambda s: composite(s, local_targets, factor), owned, has_aux=True
     )
     owned_adjoint = pullback(jnp.ones((), jnp.float32))[0]
-    adjoint = lax.all_to_all(owned_adjoint, "slab", split_axis=1, concat_axis=2, tiled=True)[
-        :, 0, :
-    ]
+    adjoint = stacked_exchange(owned_adjoint, "slab", 1, 2)[:, 0, :]
     grads = pull_all(adjoint)[0]
     grad_in, grad_mid, grad_out, grad_hid, grad_bout = lax.psum(
         (grads[0], grads[1], grads[2], grads[3], grads[4]), "rays"

time: 107 us -> 111 us (1.037)
  local copies, waits for them, and re-layouts: 11.1 us -> 15.1 us
    unnamed x36 -> x43, local copies, waits for them, and re-layouts: 7.28 us -> 11.3 us
where the time goes in v1:
time: 111 us
  waiting for transfers between devices  36.9 us (33%)
  matrix products  25.1 us (23%)
  local copies, waits for them, and re-layouts  15.1 us (14%)
  between operations  14.4 us (13%)
  starting transfers between devices  10.9 us (10%)
  blocking collectives  6.94 us (6%)
  other arithmetic  1.55 us (1%)
    psum x1, waiting for transfers between devices, shards(): lax.psum((grads[0], grads[1], grads[2], grads[3], grads[4]), 'rays')  23.7 us
    dot_general x8, matrix products, hidden_layer(): return jax.nn.softplus(jnp.dot(hidden, weight, precision=HIGH) + bias)  14.4 us
    unnamed x43, local copies, waits for them, and re-layouts  11.3 us
    all_to_all x1, starting transfers between devices, shards(): lax.all_to_all(seg[:, None, :], 'slab', split_axis=2, concat_axis=1, tile...  7.31 us
    psum x1, blocking collectives, shards(): lax.psum((grads[0], grads[1], grads[2], grads[3], grads[4]), 'rays')  6.94 us
    all_to_all x1, waiting for transfers between devices, shards(): lax.all_to_all(seg[:, None, :], 'slab', split_axis=2, concat_axis=1, tile...  6.88 us
    all_to_all x1, waiting for transfers between devices, stacked_exchange(): pieces = lax.all_to_all(pieces, axis, split_axis=0, concat_axis=0)  6.27 us
    dot_general x3, matrix products, head(): jnp.einsum('ch,nh->cn', w_out, hidden, precision=HIGH) + b_out[:, None]  5.6 us
  transfers between devices with their start and end apart: 3, of which 3 were waited for; matrix products, arithmetic and copies ran while one was open for 2% of the time, Pallas kernels for 0%

profile of v1, /device:TPU:0, one launch (start us, length us, event | category | flops | bytes accessed | tf_op | source)
XLA Modules:
  0.0 110.8 jit_solution(17583533350170487881)
XLA Ops:
  7.2 0.7 copy-done.9
  7.9 0.7 copy-done.3
  8.7 0.7 copy-done.4
  9.4 5.2 %fusion.76 = (f32[1024,128]{0,1:T(8,128)S(1)}, f32[1024,128]{0,1:T(8,128)S(1)}) fusion(f32[1,3,128]{2,0,1:T(1,128)S(1)} %copy-done.4, f32[1,3,8,128]{3,2,1,0:T(8,128)S(1)} %add_bitcast_fusion.1), kind=kOutput, calls=%fused_computation.158 | convolution fusion | flops 4718592 | bytes 1062400 | tf_op jit(solution)/shard_map/dk,dn->nk/dot_general | solution.py:26
  14.6 1.8 %convolution_add_fusion.2 = f32[1024,256]{1,0:T(8,128)S(1)} fusion(f32[1024,128]{0,1:T(8,128)S(1)} %get-tuple-element.64, f32[1024,128]{0,1:T(8,128)S(1)} %get-tuple-element.63, f32[256]{0:T(256)S(1)} %bitcast.169, f32[1,256,256]{2,1,0:T(8,128)S(1)} %copy-done), kind=kOutput, calls=%fused_computation.14 | convolution fusion | flops 805830656 | bytes 2360320 | tf_op jit(solution)/shard_map/jvp()/dot_general | solution.py:31
  16.4 1.4 %convolution_add_fusion.1 = f32[1024,256]{1,0:T(8,128)S(1)} fusion(f32[1024,256]{1,0:T(8,128)S(1)} %convolution_add_fusion.2, f32[256]{0:T(256)S(1)} %bitcast.178, f32[1,2,256,256]{3,2,1,0:T(8,128)S(1)} %copy-done.7), kind=kOutput, calls=%fused_computation.13 | convolution fusion | flops 807141376 | bytes 2360320 | tf_op jit(solution)/shard_map/jvp()/dot_general | solution.py:31
  17.9 1.5 %convolution_add_fusion = f32[1024,256]{1,0:T(8,128)S(1)} fusion(f32[1024,256]{1,0:T(8,128)S(1)} %convolution_add_fusion.1, f32[256]{0:T(256)S(1)} %bitcast.177, f32[1,2,256,256]{3,2,1,0:T(8,128)S(1)} %copy-done.7), kind=kOutput, calls=%fused_computation.12 | convolution fusion | flops 807141376 | bytes 2360320 | tf_op jit(solution)/shard_map/jvp()/dot_general | solution.py:31
  19.4 0.7 copy-done.10
  20.0 1.5 %fusion = f32[4,1024]{1,0:T(4,128)S(1)} fusion(f32[1024,256]{1,0:T(8,128)S(1)} %convolution_add_fusion, f32[4]{0:T(128)S(1)} %bitcast.179, f32[1,4,256]{2,1,0:T(4,128)S(1)} %copy-done.8), kind=kOutput, calls=%fused_computation.19 | convolution fusion | flops 14159872 | bytes 1069072 | tf_op jit(solution)/shard_map/jvp(ch,nh->cn)/dot_general | solution.py:37
  21.6 0.6 copy-done.5
  22.4 0.8 copy.30
  23.1 7.3 %all-to-all-start = ((f32[4,1,128]{0,1,2:T(1,128)}), f32[4,1,128]{0,1,2:T(1,128)S(1)}, u32[]{:S(2)}, u32[]{:S(2)}) async-start(f32[4,1,128]{0,1,2:T(1,128)} %bitcast.13), calls=%async_computation | async-start | bytes 131072 | tf_op jit(solution)/shard_map/all_to_all | solution.py:76
  30.5 6.9 %all-to-all-done = f32[4,1,128]{0,1,2:T(1,128)S(1)} async-done(((f32[4,1,128]{0,1,2:T(1,128)}), f32[4,1,128]{0,1,2:T(1,128)S(1)}, u32[]{:S(2)}, u32[]{:S(2)}) %all-to-all-start) | async-done | bytes 2080 | tf_op jit(solution)/shard_map/all_to_all | solution.py:76
  37.3 1.8 %slice_reduce_fusion = f32[128]{0:T(128)S(1)} fusion(f32[4,1,128]{0,1,2:T(1,128)S(1)} %all-to-all-done), kind=kLoop, calls=%fused_computation.44 | loop fusion | bytes 1024 | tf_op jit(solution)/shard_map/jvp()/slice | solution.py:57
  39.6 0.7 copy-done.6
  40.6 0.6 constant_dynamic-update-slice_fusion.7
  41.2 0.6 constant_dynamic-update-slice_fusion.6
  41.8 0.6 constant_dynamic-update-slice_fusion.5
  45.2 3.3 %all-to-all-start.1 = ((f32[8,4,1,16]{3,1,2,0:T(4,128)}), f32[8,4,1,16]{3,1,2,0:T(4,128)S(1)}, u32[]{:S(2)}, u32[]{:S(2)}) async-start(f32[8,4,1,16]{3,1,2,0:T(4,128)} %constant_dynamic-update-slice_fusion), calls=%async_computation.1 | async-start | bytes 32768 | tf_op jit(solution)/shard_map/all_to_all | solution.py:16
  48.8 6.3 %all-to-all-done.1 = f32[8,4,1,16]{3,1,2,0:T(4,128)S(1)} async-done(((f32[8,4,1,16]{3,1,2,0:T(4,128)}), f32[8,4,1,16]{3,1,2,0:T(4,128)S(1)}, u32[]{:S(2)}, u32[]{:S(2)}) %all-to-all-start.1) | async-done | bytes 2080 | tf_op jit(solution)/shard_map/all_to_all | solution.py:16
  55.5 3.0 %fusion.82 = (f32[256]{0:T(256)S(1)}, f32[1024,256]{1,0:T(8,128)S(1)}) fusion(f32[1024,256]{1,0:T(8,128)} %copy-done.13, f32[1,4,256]{2,1,0:T(4,128)S(1)} %copy-done.8, f32[1,1024]{1,0:T(1,128)S(1)} %fusion.36, f32[3,1024]{1,0:T(4,128)S(1)} %get-tuple-element.65), kind=kOutput, calls=%fused_computation.164 | convolution fusion | flops 15994624 | bytes 2118656 | tf_op jit(solution)/shard_map/transpose(jvp(ch,nh->cn))/dot_general | solution.py:37
  58.5 2.3 %convolution_bitcast_fusion.1 = f32[1,256,256]{2,1,0:T(8,128)S(1)} fusion(f32[1024,256]{1,0:T(8,128)S(1)} %get-tuple-element.88, f32[1024,256]{1,0:T(8,128)S(1)} %copy-done.12), kind=kOutput, calls=%fused_computation.16 | convolution fusion | flops 806879232 | bytes 2359296 | tf_op jit(solution)/shard_map/transpose(jvp())/dot_general | solution.py:31
  60.8 1.7 %fusion.81 = (f32[256]{0:T(256)S(1)}, f32[1024,256]{1,0:T(8,128)S(1)}) fusion(f32[1024,256]{1,0:T(8,128)S(1)} %copy-done.12, f32[1024,256]{1,0:T(8,128)S(1)} %get-tuple-element.88, f32[1,2,256,256]{3,2,1,0:T(8,128)S(1)} %copy-done.7), kind=kOutput, calls=%fused_computation.163 | convolution fusion | flops 808713984 | bytes 3408896 | tf_op jit(solution)/shard_map/transpose(jvp())/dot_general | solution.py:31
  62.5 2.3 %convolution_bitcast_fusion = f32[1,256,256]{2,1,0:T(8,128)S(1)} fusion(f32[1024,256]{1,0:T(8,128)S(1)} %get-tuple-element.86, f32[1024,256]{1,0:T(8,128)S(1)} %convolution_add_fusion.2), kind=kOutput, calls=%fused_computation.15 | convolution fusion | flops 806879232 | bytes 2359296 | tf_op jit(solution)/shard_map/transpose(jvp())/dot_general | solution.py:31
  64.7 1.7 %fusion.80 = (f32[256]{0:T(256)S(1)}, f32[1024,256]{1,0:T(8,128)S(1)}) fusion(f32[1024,256]{1,0:T(8,128)S(1)} %convolution_add_fusion.2, f32[1024,256]{1,0:T(8,128)S(1)} %get-tuple-element.86, f32[1,2,256,256]{3,2,1,0:T(8,128)S(1)} %copy-done.7), kind=kOutput, calls=%fused_computation.162 | convolution fusion | flops 808713984 | bytes 3408896 | tf_op jit(solution)/shard_map/transpose(jvp())/dot_general | solution.py:31
  66.4 1.7 %convolution_bitcast_fusion.2 = f32[1,256,256]{2,1,0:T(8,128)} fusion(f32[1024,256]{1,0:T(8,128)S(1)} %get-tuple-element.84, f32[1024,128]{0,1:T(8,128)S(1)} %get-tuple-element.64, f32[1024,128]{0,1:T(8,128)S(1)} %get-tuple-element.63), kind=kOutput, calls=%fused_computation.17 | convolution fusion | flops 805568512 | bytes 2359296 | tf_op jit(solution)/shard_map/transpose(jvp())/dot_general | solution.py:31
  68.2 0.8 add_bitcast_fusion
  69.7 1.1 convolution_bitcast_fusion.3
  70.8 6.9 %all-reduce.9 = (f32[1,4,256]{2,1,0:T(4,128)}, f32[1,3,256]{2,0,1:T(1,128)}, f32[1,4]{1,0:T(1,128)}) all-reduce(f32[1,4,256]{2,1,0:T(4,128)S(1)} %convolution_bitcast_fusion.3, f32[1,3,256]{2,0,1:T(1,128)S(1)} %broadcast_in_dim.83, f32[1,4]{1,0:T(1,128)S(1)} %bitcast.173), channel_id=1, replica_groups=mesh['slab'=8,'rays'=4] {'rays'}, use_global_device_ids=true, to_apply=%region_13.15 | all-reduce | flops 1796 | bytes 14368 | tf_op jit(solution)/shard_map/psum | solution.py:83
  77.7 23.7 %all-reduce.13.cloned.1.call-done = (f32[1,256,256]{2,1,0:T(8,128)}, f32[1,2,256,256]{3,2,1,0:T(8,128)}) async-done(((f32[1,256,256]{2,1,0:T(8,128)}, f32[1,2,256,256]{3,2,1,0:T(8,128)}), (f32[1,256,256]{2,1,0:T(8,128)}, f32[1,2,256,256]{3,2,1,0:T(8,128)})) %all-reduce.13.cloned.1.call-update) | async-done | bytes 786448 | tf_op jit(solution)/shard_map/psum | solution.py:83
  101.5 1.7 %copy.83 = f32[1,256,256]{2,1,0:T(8,128)} copy(f32[1,256,256]{2,1,0:T(8,128)} %get-tuple-element.92) | data formatting | bytes 524288
  103.2 0.8 copy.84
  (82 shorter events, 5.2 us)
Async XLA Ops:
  7.2 7.4 %copy-start = (f32[1,256,256]{2,1,0:T(8,128)S(1)}, f32[1,256,256]{2,1,0:T(8,128)}, u32[]{:S(2)}) copy-start(f32[1,256,256]{2,1,0:T(8,128)} %param.15) | copy-start | bytes 786436
  7.2 0.7 copy-start.9
  7.2 0.7 copy-start.2
  7.9 0.7 copy-start.3
  8.7 0.7 copy-start.4
  14.5 1.8 %copy-start.7 = (f32[1,2,256,256]{3,2,1,0:T(8,128)S(1)}, f32[1,2,256,256]{3,2,1,0:T(8,128)}, u32[]{:S(2)}) copy-start(f32[1,2,256,256]{3,2,1,0:T(8,128)} %param.16) | copy-start | bytes 1572868
  17.8 1.5 %copy-start.11 = (f32[1024,256]{1,0:T(8,128)}, f32[1024,256]{1,0:T(8,128)S(1)}, u32[]{:S(2)}) copy-start(f32[1024,256]{1,0:T(8,128)S(1)} %convolution_add_fusion.1) | copy-start | bytes 3145732
  17.9 1.5 %copy-start.8 = (f32[1,4,256]{2,1,0:T(4,128)S(1)}, f32[1,4,256]{2,1,0:T(4,128)}, u32[]{:S(2)}) copy-start(f32[1,4,256]{2,1,0:T(4,128)} %param.17) | copy-start | bytes 12292
  19.3 2.2 %copy-start.13 = (f32[1024,256]{1,0:T(8,128)}, f32[1024,256]{1,0:T(8,128)S(1)}, u32[]{:S(2)}) copy-start(f32[1024,256]{1,0:T(8,128)S(1)} %convolution_add_fusion) | copy-start | bytes 3145732
  19.4 0.7 copy-start.10
  21.6 0.7 copy-start.5
  23.1 14.2 %all-to-all-start = ((f32[4,1,128]{0,1,2:T(1,128)}), f32[4,1,128]{0,1,2:T(1,128)S(1)}, u32[]{:S(2)}, u32[]{:S(2)}) async-start(f32[4,1,128]{0,1,2:T(1,128)} %bitcast.13), calls=%async_computation | async-start | bytes 131072 | tf_op jit(solution)/shard_map/all_to_all | solution.py:76
  39.6 0.7 copy-start.6
  45.2 9.9 %all-to-all-start.1 = ((f32[8,4,1,16]{3,1,2,0:T(4,128)}), f32[8,4,1,16]{3,1,2,0:T(4,128)S(1)}, u32[]{:S(2)}, u32[]{:S(2)}) async-start(f32[8,4,1,16]{3,1,2,0:T(4,128)} %constant_dynamic-update-slice_fusion), calls=%async_computation.1 | async-start | bytes 32768 | tf_op jit(solution)/shard_map/all_to_all | solution.py:16
  48.6 52.9 %all-reduce.13.cloned.1.call-start = ((), (), s32[]{:S(2)}) async-start(), calls=%async_computation.2 | async-start | bytes 1572864 | tf_op jit(solution)/shard_map/psum | solution.py:83
  55.4 3.1 %copy-start.12 = (f32[1024,256]{1,0:T(8,128)S(1)}, f32[1024,256]{1,0:T(8,128)}, u32[]{:S(2)}) copy-start(f32[1024,256]{1,0:T(8,128)} %copy-done.11) | copy-start | bytes 3145732
  68.2 1.6 %copy-start.14 = (f32[1024,256]{1,0:T(8,128)S(1)}, f32[1024,256]{1,0:T(8,128)}, u32[]{:S(2)}) copy-start(f32[1024,256]{1,0:T(8,128)} %copy-done.13) | copy-start | bytes 3145732
  101.5 1.7 %copy-start.1 = (f32[1,2,256,256]{3,2,1,0:T(8,128)S(1)}, f32[1,2,256,256]{3,2,1,0:T(8,128)}, u32[]{:S(2)}) copy-start(f32[1,2,256,256]{3,2,1,0:T(8,128)} %get-tuple-element.93) | copy-start | bytes 1572868
Sparse Core Ops, SparseCore 0:
  69.1 32.2 all-reduce.12
